TPU v7x, 32 devices: a whole 2x2x4 slice. The times are simulated.
32 devices in a mesh: rep: 2 (over y), head: 4 (over z), ctx: 4 (over x, core).
Axes of the slice: x: 2, y: 2, z: 4, core: 2. Of those that a mesh axis runs over, the one named last changes fastest.
Arguments:
- queries: bfloat16 [8, 512, 8192], P(('rep', 'ctx'), 'head'), parts along dimension 0, may hold values from -6 to 6
- keys: bfloat16 [8, 512, 8192], P(('rep', 'ctx'), 'head'), parts along dimension 0, may hold values from -6 to 6
- values: bfloat16 [8, 512, 8192], P(('rep', 'ctx'), 'head'), parts along dimension 0, may hold values from -6 to 6
- gain: float32 [8192], replicated, may hold values from 0.5 to 1.5
Outputs:
- normed: bfloat16 [8, 512, 8192], P(('rep', 'ctx'), 'head'), parts along dimension 0
There are 2 independent parts, one for each index of `rep`. A program takes and returns all parts, laid end to end along the dimension named above; an argument that names none is the same for every part. Nothing has to cross between parts.
All inputs are finite; a program needn't handle non-finite values.
Results may differ from a plain program's by a relative error of at most 0.0059.
Values may be sent and summed in bfloat16 or wider, within the bound.
No kernel may reach another device: no remote copies, remote signals or barrier semaphores. Data moves between devices by JAX's collectives and lax.ppermute only.
A program may use at most 128 MiB of HBM per device.

v0:
```python
import jax
import jax.numpy as jnp
from jax import lax
from jax.sharding import PartitionSpec as P

DH = 128


def entering(part, axis, combine, identity):
    place = lax.axis_index(axis)
    gathered = lax.all_gather(part, axis)
    state = jnp.zeros_like(part) + jnp.asarray(identity, part.dtype)

    def one(step, state):
        return combine(state, lax.dynamic_index_in_dim(gathered, step, 0, False))

    return lax.fori_loop(0, place, one, state)


def block_attention(query_blk, key_blk, value_blk, state_blk):
    length = query_blk.shape[-2]
    causal = jnp.arange(length)[:, None] >= jnp.arange(length)[None, :]
    scores = jnp.einsum(
        "...htd,...hsd->...hts", query_blk, key_blk, preferred_element_type=jnp.float32
    )
    scores = jnp.where(causal, scores, jnp.float32(0.0)).astype(jnp.bfloat16)
    local_part = jnp.einsum(
        "...hts,...hsd->...htd", scores, value_blk, preferred_element_type=jnp.float32
    )
    carried = jnp.einsum(
        "...htd,...hde->...hte", query_blk, state_blk, preferred_element_type=jnp.float32
    )
    return (local_part + carried).astype(jnp.bfloat16)


def activate(rows):
    return jax.nn.silu(rows.astype(jnp.float32)).astype(jnp.bfloat16)


def row_norm(attn, gain):
    wide = attn.astype(jnp.float32)
    mean_sq = jnp.mean(wide * wide, axis=1, keepdims=True)
    return (wide * lax.rsqrt(mean_sq + 1e-06) * gain[None, :]).astype(jnp.bfloat16)


def body(queries, keys, values, gain):
    tok_rows = queries.shape[1]
    width = queries.shape[2]
    q_rows = queries.reshape(tok_rows, width)
    k_rows = keys.reshape(tok_rows, width)
    v_rows = values.reshape(tok_rows, width)
    head_q, head_k, head_v = (
        lax.all_to_all(q_rows, "head", split_axis=1, concat_axis=0, tiled=True),
        lax.all_to_all(k_rows, "head", split_axis=1, concat_axis=0, tiled=True),
        lax.all_to_all(v_rows, "head", split_axis=1, concat_axis=0, tiled=True),
    )
    span = head_q.shape[0]
    local_cols = head_q.shape[1]
    local_heads = local_cols // DH
    blocks = span // tok_rows
    query_hb = activate(head_q).reshape(blocks, tok_rows, local_heads, DH).transpose(0, 2, 1, 3)
    key_hb = activate(head_k).reshape(blocks, tok_rows, local_heads, DH).transpose(0, 2, 1, 3)
    value_hb = head_v.reshape(blocks, tok_rows, local_heads, DH).transpose(0, 2, 1, 3)
    block_states = jnp.einsum(
        "bhtd,bhte->bhde", key_hb, value_hb, preferred_element_type=jnp.float32
    )
    stretch_total = jnp.sum(block_states, axis=0)
    earlier = entering(
        stretch_total, "ctx", lambda first, second: first + second, jnp.zeros_like(stretch_total)
    )
    running = jnp.cumsum(block_states, axis=0)
    within = jnp.concatenate([jnp.zeros_like(running[:1]), running[:-1]], axis=0)
    states = (earlier[None] + within).astype(jnp.bfloat16)
    attn = block_attention(query_hb, key_hb, value_hb, states)
    attn = attn.transpose(0, 2, 1, 3).reshape(span, local_cols)
    back = lax.all_to_all(attn, "head", split_axis=0, concat_axis=1, tiled=True)
    normed = row_norm(back, gain)
    return normed.reshape(1, tok_rows, width)


def solution(mesh):
    return jax.shard_map(
        body,
        mesh=mesh,
        in_specs=(
            P(("rep", "ctx"), "head", None),
            P(("rep", "ctx"), "head", None),
            P(("rep", "ctx"), "head", None),
            P(),
        ),
        out_specs=P(("rep", "ctx"), "head", None),
        check_vma=False,
    )
```

profile of v0, /device:TPU:2, one launch (start us, length us, event | category | flops | bytes accessed | tf_op | source)
XLA Modules:
  0.0 270.1 jit_solution(5377043979471332079)
XLA Ops:
  6.5 4.1 %copy.18 = bf16[1,128,8192]{1,2,0:T(8,128)(2,1)} copy(bf16[1,128,8192]{2,1,0:T(8,128)(2,1)} %param.7) | data formatting | bytes 4194304 | tf_op args[1]
  10.6 4.9 %all-to-all-start.1 = ((bf16[128,4,2048]{0,2,1:T(8,128)(2,1)}), bf16[128,4,2048]{0,2,1:T(8,128)(2,1)S(1)}, u32[]{:S(2)}, u32[]{:S(2)}) async-start(bf16[128,4,2048]{0,2,1:T(8,128)(2,1)} %bitcast.47), calls=%async_computation.1 | async-start | bytes 4194304 | tf_op jit(solution)/shard_map/all_to_all | solution.py:54
  15.5 4.1 %copy.31 = bf16[1,128,8192]{1,2,0:T(8,128)(2,1)} copy(bf16[1,128,8192]{2,1,0:T(8,128)(2,1)} %param.8) | data formatting | bytes 4194304 | tf_op jit(solution)/shard_map/all_to_all | solution.py:55
  19.5 44.1 %all-to-all-done.1 = bf16[128,4,2048]{0,2,1:T(8,128)(2,1)S(1)} async-done(((bf16[128,4,2048]{0,2,1:T(8,128)(2,1)}), bf16[128,4,2048]{0,2,1:T(8,128)(2,1)S(1)}, u32[]{:S(2)}, u32[]{:S(2)}) %all-to-all-start.1) | async-done | bytes 2097184 | tf_op jit(solution)/shard_map/all_to_all | solution.py:54
  63.7 4.4 %all-to-all-start.2 = ((bf16[128,4,2048]{0,2,1:T(8,128)(2,1)}), bf16[128,4,2048]{0,2,1:T(8,128)(2,1)}, u32[]{:S(2)}, u32[]{:S(2)}) async-start(bf16[128,4,2048]{0,2,1:T(8,128)(2,1)} %bitcast.46), calls=%async_computation.2 | async-start | bytes 4194304 | tf_op jit(solution)/shard_map/all_to_all | solution.py:55
  68.1 0.0 all-gather.3.cloned.1.call-start
  68.1 2.2 convert_element_type.92
  70.4 45.5 %all-to-all-done.2 = bf16[128,4,2048]{0,2,1:T(8,128)(2,1)} async-done(((bf16[128,4,2048]{0,2,1:T(8,128)(2,1)}), bf16[128,4,2048]{0,2,1:T(8,128)(2,1)}, u32[]{:S(2)}, u32[]{:S(2)}) %all-to-all-start.2) | async-done | bytes 2097184 | tf_op jit(solution)/shard_map/all_to_all | solution.py:55
  115.9 0.0 copy-start
  115.9 7.3 %fusion.13 = (f32[16,128,128]{2,1,0:T(8,128)}, f32[4,16,128,128]{3,2,1,0:T(8,128)}) fusion(bf16[4,16,128,128]{2,3,1,0:T(8,128)(2,1)} %bitcast.14, f32[4,128,16,128]{1,3,2,0:T(8,128)} %bitcast.51), kind=kOutput, calls=%fused_computation.19 | convolution fusion | flops 274464768 | bytes 11534336 | tf_op jit(solution)/shard_map/bhtd,bhte->bhde/dot_general | solution.py:64
  123.2 0.0 all-gather.3.cloned.1.call-update
  123.2 0.0 copy-done
  123.2 2.4 copy.17
  125.7 3.6 %all-to-all-start = ((bf16[128,4,2048]{0,2,1:T(8,128)(2,1)}), bf16[128,4,2048]{0,2,1:T(8,128)(2,1)S(1)}, u32[]{:S(2)}, u32[]{:S(2)}) async-start(bf16[128,4,2048]{0,2,1:T(8,128)(2,1)} %bitcast.45), calls=%async_computation | async-start | bytes 4194304 | tf_op jit(solution)/shard_map/all_to_all | solution.py:53
  129.3 3.1 %fusion.14 = f32[4,16,128,128]{3,2,1,0:T(8,128)S(1)} fusion(f32[4,16,128,128]{3,2,1,0:T(8,128)} %get-tuple-element.38), kind=kOutput, calls=%fused_computation.20 | output fusion | flops 3145728 | bytes 8388608 | tf_op jit(solution)/shard_map/jit(cumsum)/reduce_window_sum | solution.py:71
  132.5 2.0 slice.4
  134.5 42.5 %all-to-all-done = bf16[128,4,2048]{0,2,1:T(8,128)(2,1)S(1)} async-done(((bf16[128,4,2048]{0,2,1:T(8,128)(2,1)}), bf16[128,4,2048]{0,2,1:T(8,128)(2,1)S(1)}, u32[]{:S(2)}, u32[]{:S(2)}) %all-to-all-start) | async-done | bytes 2097184 | tf_op jit(solution)/shard_map/all_to_all | solution.py:53
  176.9 2.2 convert_element_type.91
  179.2 10.1 %fusion.8 = f32[4,16,128,128]{2,3,1,0:T(8,128)} fusion(bf16[4,16,128,128]{2,3,1,0:T(8,128)(2,1)} %bitcast.14, pred[128,128]{1,0:T(8,128)(4,1)S(1)} %iota_compare_fusion, f32[4,128,16,128]{1,3,2,0:T(8,128)} %bitcast.49, f32[4,128,16,128]{1,3,2,0:T(8,128)} %bitcast.52), kind=kOutput, calls=%fused_computation.14 | convolution fusion | flops 549453824 | bytes 14696448 | tf_op jit(solution)/shard_map/...hts,...hsd->...htd/dot_general | solution.py:27
  189.3 0.0 all-gather.3.cloned.1.call-done
  189.3 0.1 broadcast_in_dim.19
  189.4 3.0 %while.10 = (s32[]{:T(128)}, f32[16,128,128]{2,1,0:T(8,128)S(1)}, s32[]{:T(128)}, f32[4,16,128,128]{3,2,1,0:T(8,128)}, s32[]{:T(128)}, /*index=5*/s32[]{:T(128)}, s32[]{:T(128)}) while((s32[]{:T(128)}, f32[16,128,128]{2,1,0:T(8,128)S(1)}, s32[]{:T(128)}, f32[4,16,128,128]{3,2,1,0:T(8,128)}, s32[]{:T(128)}, /*index=5*/s32[]{:T(128)}, ...), condition=%wide.region_2.3_spmd, body=%wide.region_1.2_spmd.sunk | while | flops 262149 | bytes 3145843 | solution.py:17
  189.4 1.5 bitcast_add_fusion.2
  190.9 1.5 bitcast_add_fusion.2
  192.4 6.2 %add_convert_fusion = bf16[4,16,128,128]{2,3,1,0:T(8,128)(2,1)S(1)} fusion(f32[4,16,128,128]{2,3,1,0:T(8,128)} %fusion.8, f32[3,16,128,128]{3,2,1,0:T(8,128)} %slice.4, f32[16,128,128]{2,1,0:T(8,128)S(1)} %get-tuple-element.28, f32[4,128,16,128]{1,3,2,0:T(8,128)} %bitcast.50), kind=kOutput, calls=%fused_computation.3 | convolution fusion | flops 277872640 | bytes 14680064 | tf_op jit(solution)/shard_map/...htd,...hde->...hte/dot_general | solution.py:30
  198.6 51.7 %all_to_all.55 = bf16[4,128,2048]{1,2,0:T(8,128)(2,1)S(1)} all-to-all(bf16[4,128,2048]{1,2,0:T(8,128)(2,1)S(1)} %bitcast.53), channel_id=1, replica_groups=mesh['rep'=2,'head'=4,'ctx'=4] {'head'}, dimensions={0} | all-to-all | bytes 4194304 | tf_op jit(solution)/shard_map/all_to_all | solution.py:76
  250.3 2.2 convert_element_type.93
  252.5 0.0 copy-start.1
  252.5 5.6 %copy.32 = f32[1,128,8192]{2,1,0:T(8,128)} copy(f32[1,128,8192]{1,2,0:T(8,128)} %bitcast.44) | data formatting | bytes 8388608 | tf_op jit(solution)/shard_map/convert_element_type | solution.py:41
  258.1 1.1 multiply_reduce_fusion
  259.2 0.0 copy-done.1
  259.2 4.0 %multiply_convert_fusion = bf16[1,128,8192]{2,1,0:T(8,128)(2,1)} fusion(f32[1,128,8192]{2,1,0:T(8,128)} %copy.32, f32[8192]{0:T(1024)S(1)} %copy-done.1, f32[128]{0:T(128)S(1)} %add_rsqrt_fusion), kind=kLoop, calls=%fused_computation.1 | loop fusion | flops 3145728 | bytes 6324736 | tf_op jit(solution)/shard_map/convert_element_type | solution.py:43
  (2 shorter events, 0.0 us)
Async XLA Ops:
  10.6 53.1 %all-to-all-start.1 = ((bf16[128,4,2048]{0,2,1:T(8,128)(2,1)}), bf16[128,4,2048]{0,2,1:T(8,128)(2,1)S(1)}, u32[]{:S(2)}, u32[]{:S(2)}) async-start(bf16[128,4,2048]{0,2,1:T(8,128)(2,1)} %bitcast.47), calls=%async_computation.1 | async-start | bytes 4194304 | tf_op jit(solution)/shard_map/all_to_all | solution.py:54
  63.7 52.2 %all-to-all-start.2 = ((bf16[128,4,2048]{0,2,1:T(8,128)(2,1)}), bf16[128,4,2048]{0,2,1:T(8,128)(2,1)}, u32[]{:S(2)}, u32[]{:S(2)}) async-start(bf16[128,4,2048]{0,2,1:T(8,128)(2,1)} %bitcast.46), calls=%async_computation.2 | async-start | bytes 4194304 | tf_op jit(solution)/shard_map/all_to_all | solution.py:55
  68.1 121.2 %all-gather.3.cloned.1.call-start = ((), (), s32[]{:S(2)}) async-start(), calls=%async_computation.4 | async-start | bytes 5242880 | tf_op jit(solution)/shard_map/all_gather | solution.py:11
  115.9 7.3 %copy-start = (bf16[1,128,8192]{2,1,0:T(8,128)(2,1)S(1)}, bf16[1,128,8192]{2,1,0:T(8,128)(2,1)}, u32[]{:S(2)}) copy-start(bf16[1,128,8192]{2,1,0:T(8,128)(2,1)} %param.6) | copy-start | bytes 6291460
  125.7 51.3 %all-to-all-start = ((bf16[128,4,2048]{0,2,1:T(8,128)(2,1)}), bf16[128,4,2048]{0,2,1:T(8,128)(2,1)S(1)}, u32[]{:S(2)}, u32[]{:S(2)}) async-start(bf16[128,4,2048]{0,2,1:T(8,128)(2,1)} %bitcast.45), calls=%async_computation | async-start | bytes 4194304 | tf_op jit(solution)/shard_map/all_to_all | solution.py:53
  252.5 6.7 %copy-start.1 = (f32[8192]{0:T(1024)S(1)}, f32[8192]{0:T(1024)}, u32[]{:S(2)}) copy-start(f32[8192]{0:T(1024)} %param.9) | copy-start | bytes 98308
Sparse Core Ops, SparseCore 0:
  123.3 32.4 all-gather.2
where the time goes:
time: 271 us; the launch traced here: 270 us
  waiting for transfers between devices  132 us (49%)
  blocking collectives  51.7 us (19%)
  matrix products  23.6 us (9%)
  local copies, waits for them, and re-layouts  18.3 us (7%)
  other arithmetic  17.9 us (7%)
  between operations  13.5 us (5%)
  starting transfers between devices  13 us (5%)
    all_to_all x1, blocking collectives, body(): back = lax.all_to_all(attn, 'head', split_axis=0, concat_axis=1, tiled=True)  51.7 us
    all_to_all x1, waiting for transfers between devices, body(): lax.all_to_all(v_rows, 'head', split_axis=1, concat_axis=0, tiled=True)  45.5 us
    all_to_all x1, waiting for transfers between devices, body(): lax.all_to_all(k_rows, 'head', split_axis=1, concat_axis=0, tiled=True)  44.1 us
    all_to_all x1, waiting for transfers between devices, body(): lax.all_to_all(q_rows, 'head', split_axis=1, concat_axis=0, tiled=True)  42.5 us
    dot_general x1, matrix products, block_attention(): jnp.einsum('...hts,...hsd->...htd', scores, value_blk, preferred_element_...  10.1 us
    dot_general x1, matrix products, body(): jnp.einsum('bhtd,bhte->bhde', key_hb, value_hb, preferred_element_type=jn...  7.32 us
    unnamed x6, local copies, waits for them, and re-layouts  6.5 us
    dot_general x1, matrix products, block_attention(): jnp.einsum('...htd,...hde->...hte', query_blk, state_blk, preferred_eleme...  6.17 us
  transfers between devices with their start and end apart: 4, of which 3 were waited for; matrix products, arithmetic and copies ran while one was open for 10% of the time, Pallas kernels for 0%

commit v1 on v0

--- a/solution.py
+++ b/solution.py
@@ -73,7 +73,15 @@
     states = (earlier[None] + within).astype(jnp.bfloat16)
     attn = block_attention(query_hb, key_hb, value_hb, states)
     attn = attn.transpose(0, 2, 1, 3).reshape(span, local_cols)
-    back = lax.all_to_all(attn, "head", split_axis=0, concat_axis=1, tiled=True)
+    ways, here = (lax.axis_size("head"), lax.axis_index("head"))
+    width_2 = attn.shape[0] // ways
+    turned = jnp.roll(attn, -here * width_2, axis=0)
+    got = [lax.slice_in_dim(turned, 0, width_2, axis=0)]
+    for far in range(1, ways):
+        sent = lax.slice_in_dim(turned, far * width_2, (far + 1) * width_2, axis=0)
+        got.append(lax.ppermute(sent, "head", [(d, (d + far) % ways) for d in range(ways)]))
+    line = jnp.concatenate(got[::-1], axis=1)
+    back = jnp.roll(line, (here + 1) * got[0].shape[1], axis=1)
     normed = row_norm(back, gain)
     return normed.reshape(1, tok_rows, width)
 

time: 271 us -> 263 us (0.970)
  blocking collectives: 51.7 us -> 0 us
  waiting for transfers between devices: 132 us -> 174 us
  local copies, waits for them, and re-layouts: 18.3 us -> 25.5 us
  other arithmetic: 17.9 us -> 13.2 us
  matrix products: 23.6 us -> 19.6 us
    all_to_all x1 -> x0, blocking collectives: 51.7 us -> none  [body(): back = lax.all_to_all(attn, 'head', split_axis=0, concat_axis=1, tiled=True)]
    ppermute x0 -> x3, waiting for transfers between devices: none -> 44.1 us  [body(): lax.ppermute(sent, 'head', [(d, (d + far) % ways) for d in range(ways)])]
    unnamed x6 -> x21, local copies, waits for them, and re-layouts: 6.5 us -> 16.9 us
    convert_element_type x2 -> x0, other arithmetic: 6.22 us -> none  [the longest x1 4.01 us: row_norm(): (wide * lax.rsqrt(mean_sq + 1e-06) * gain[None, :]).astype(jnp.bfloat16)]
    convert_element_type x1, local copies, waits for them, and re-layouts: 5.6 us -> 1.36 us  [block_attention(): return (local_part + carried).astype(jnp.bfloat16)]
    all_to_all x1 -> x0, local copies, waits for them, and re-layouts: 4.06 us -> none  [body(): lax.all_to_all(v_rows, 'head', split_axis=1, concat_axis=0, tiled=True)]
    reshape x0 -> x1, local copies, waits for them, and re-layouts: none -> 3.95 us  [body(): head_v.reshape(blocks, tok_rows, local_heads, DH).transpose(0, 2, 1, 3)]
    dot_general x1, matrix products: 7.32 us -> 4.37 us  [body(): jnp.einsum('bhtd,bhte->bhde', key_hb, value_hb, preferred_element_type=jn...]
  transfers between devices with their start and end apart: 4 -> 7, of which waited for: 3 -> 5; matrix products, arithmetic and copies ran while one was open for 10% -> 10% of each run, Pallas kernels for 0% -> 0%
where the time goes in v1:
time: 263 us; the launch traced here: 261 us
  waiting for transfers between devices  174 us (66%)
  local copies, waits for them, and re-layouts  25.5 us (10%)
  matrix products  19.6 us (7%)
  starting transfers between devices  14.2 us (5%)
  between operations  13.6 us (5%)
  other arithmetic  13.2 us (5%)
    ppermute x3, waiting for transfers between devices, body(): lax.ppermute(sent, 'head', [(d, (d + far) % ways) for d in range(ways)])  44.1 us
    all_to_all x1, waiting for transfers between devices, body(): lax.all_to_all(v_rows, 'head', split_axis=1, concat_axis=0, tiled=True)  44.1 us
    all_to_all x1, waiting for transfers between devices, body(): lax.all_to_all(k_rows, 'head', split_axis=1, concat_axis=0, tiled=True)  43.7 us
    all_to_all x1, waiting for transfers between devices, body(): lax.all_to_all(q_rows, 'head', split_axis=1, concat_axis=0, tiled=True)  42.5 us
    unnamed x21, local copies, waits for them, and re-layouts  16.9 us
    dot_general x1, matrix products, block_attention(): jnp.einsum('...hts,...hsd->...htd', scores, value_blk, preferred_element_...  9.27 us
    dot_general x1, matrix products, block_attention(): jnp.einsum('...htd,...hde->...hte', query_blk, state_blk, preferred_eleme...  5.94 us
  transfers between devices with their start and end apart: 7, of which 5 were waited for; matrix products, arithmetic and copies ran while one was open for 10% of the time, Pallas kernels for 0%

profile of v1, /device:TPU:2, one launch (start us, length us, event | category | flops | bytes accessed | tf_op | source)
XLA Modules:
  0.0 260.7 jit_solution(6231302050535737118)
XLA Ops:
  6.5 4.1 %copy.16 = bf16[1,128,8192]{1,2,0:T(8,128)(2,1)} copy(bf16[1,128,8192]{2,1,0:T(8,128)(2,1)} %param.8) | data formatting | bytes 4194304 | tf_op args[2]
  10.6 4.9 %all-to-all-start.2 = ((bf16[128,4,2048]{0,2,1:T(8,128)(2,1)}), bf16[128,4,2048]{0,2,1:T(8,128)(2,1)S(1)}, u32[]{:S(2)}, u32[]{:S(2)}) async-start(bf16[128,4,2048]{0,2,1:T(8,128)(2,1)} %bitcast.55), calls=%async_computation.2 | async-start | bytes 4194304 | tf_op jit(solution)/shard_map/all_to_all | solution.py:55
  15.5 4.1 %copy.13 = bf16[1,128,8192]{1,2,0:T(8,128)(2,1)} copy(bf16[1,128,8192]{2,1,0:T(8,128)(2,1)} %param.7) | data formatting | bytes 4194304 | tf_op args[1]
  19.5 44.1 %all-to-all-done.2 = bf16[128,4,2048]{0,2,1:T(8,128)(2,1)S(1)} async-done(((bf16[128,4,2048]{0,2,1:T(8,128)(2,1)}), bf16[128,4,2048]{0,2,1:T(8,128)(2,1)S(1)}, u32[]{:S(2)}, u32[]{:S(2)}) %all-to-all-start.2) | async-done | bytes 2097184 | tf_op jit(solution)/shard_map/all_to_all | solution.py:55
  63.7 0.0 copy-start
  63.7 1.3 copy-done
  65.0 3.6 %all-to-all-start.1 = ((bf16[128,4,2048]{0,2,1:T(8,128)(2,1)}), bf16[128,4,2048]{0,2,1:T(8,128)(2,1)S(1)}, u32[]{:S(2)}, u32[]{:S(2)}) async-start(bf16[128,4,2048]{0,2,1:T(8,128)(2,1)} %bitcast.54), calls=%async_computation.1 | async-start | bytes 4194304 | tf_op jit(solution)/shard_map/all_to_all | solution.py:54
  68.6 0.0 all-gather.3.cloned.1.call-start
  68.6 3.9 %copy.17 = bf16[4,128,16,128]{3,1,2,0:T(8,128)(2,1)} copy(bf16[4,128,16,128]{1,3,2,0:T(8,128)(2,1)} %bitcast.53) | data formatting | bytes 4194304 | tf_op jit(solution)/shard_map/reshape | solution.py:63
  72.6 43.7 %all-to-all-done.1 = bf16[128,4,2048]{0,2,1:T(8,128)(2,1)S(1)} async-done(((bf16[128,4,2048]{0,2,1:T(8,128)(2,1)}), bf16[128,4,2048]{0,2,1:T(8,128)(2,1)S(1)}, u32[]{:S(2)}, u32[]{:S(2)}) %all-to-all-start.1) | async-done | bytes 2097184 | tf_op jit(solution)/shard_map/all_to_all | solution.py:54
  116.3 0.0 copy-start.3
  116.3 0.3 convert_element_type.64
  116.5 0.0 copy-start.1
  116.6 2.1 copy-done.3
  118.7 0.0 copy-start.2
  118.7 4.4 %fusion.24 = (f32[16,128,128]{2,1,0:T(8,128)}, f32[4,16,128,128]{3,2,1,0:T(8,128)}) fusion(bf16[4,128,16,128]{3,1,2,0:T(8,128)(2,1)S(1)} %copy-done.3, f32[4,128,16,128]{1,3,2,0:T(8,128)S(1)} %bitcast.59), kind=kOutput, calls=%fused_computation.39 | convolution fusion | flops 274464768 | bytes 11534336 | tf_op jit(solution)/shard_map/bhtd,bhte->bhde/dot_general | solution.py:64
  123.1 0.0 copy-done.1
  123.1 0.0 all-gather.3.cloned.1.call-update
  123.1 0.0 copy-done.2
  123.1 2.4 copy.12
  125.5 3.6 %all-to-all-start = ((bf16[128,4,2048]{0,2,1:T(8,128)(2,1)}), bf16[128,4,2048]{0,2,1:T(8,128)(2,1)S(1)}, u32[]{:S(2)}, u32[]{:S(2)}) async-start(bf16[128,4,2048]{0,2,1:T(8,128)(2,1)} %bitcast.52), calls=%async_computation | async-start | bytes 4194304 | tf_op jit(solution)/shard_map/all_to_all | solution.py:53
  129.2 3.1 %fusion.25 = f32[4,16,128,128]{3,2,1,0:T(8,128)S(1)} fusion(f32[4,16,128,128]{3,2,1,0:T(8,128)} %get-tuple-element.41), kind=kOutput, calls=%fused_computation.40 | output fusion | flops 3145728 | bytes 8388608 | tf_op jit(solution)/shard_map/jit(cumsum)/reduce_window_sum | solution.py:71
  132.4 2.0 slice.20
  134.3 42.5 %all-to-all-done = bf16[128,4,2048]{0,2,1:T(8,128)(2,1)S(1)} async-done(((bf16[128,4,2048]{0,2,1:T(8,128)(2,1)}), bf16[128,4,2048]{0,2,1:T(8,128)(2,1)S(1)}, u32[]{:S(2)}, u32[]{:S(2)}) %all-to-all-start) | async-done | bytes 2097184 | tf_op jit(solution)/shard_map/all_to_all | solution.py:53
  176.8 2.2 convert_element_type.63
  179.0 9.3 %fusion.7 = f32[4,16,128,128]{3,2,1,0:T(8,128)} fusion(bf16[4,128,16,128]{3,1,2,0:T(8,128)(2,1)} %copy.17, pred[128,128]{1,0:T(8,128)(4,1)S(1)} %iota_compare_fusion, f32[4,128,16,128]{1,3,2,0:T(8,128)} %bitcast.61, f32[4,128,16,128]{1,3,2,0:T(8,128)} %bitcast.60), kind=kOutput, calls=%fused_computation.18 | convolution fusion | flops 549453824 | bytes 14696448 | tf_op jit(solution)/shard_map/...hts,...hsd->...htd/dot_general | solution.py:27
  188.3 0.0 all-gather.3.cloned.1.call-done
  188.3 0.1 broadcast_in_dim.19
  188.4 3.2 %while.10 = (s32[]{:T(128)}, f32[16,128,128]{2,1,0:T(8,128)S(1)}, s32[]{:T(128)}, f32[4,16,128,128]{3,2,1,0:T(8,128)}, s32[]{:T(128)}, /*index=5*/s32[]{:T(128)}, s32[]{:T(128)}) while((s32[]{:T(128)}, f32[16,128,128]{2,1,0:T(8,128)S(1)}, s32[]{:T(128)}, f32[4,16,128,128]{3,2,1,0:T(8,128)}, s32[]{:T(128)}, /*index=5*/s32[]{:T(128)}, ...), condition=%wide.region_2.3_spmd, body=%wide.region_1.2_spmd.sunk | while | flops 262149 | bytes 3145843 | solution.py:17
  188.4 1.5 bitcast_add_fusion.2
  190.0 1.5 bitcast_add_fusion.2
  191.6 5.9 %fusion.18 = bf16[4,128,16,128]{3,1,2,0:T(8,128)(2,1)S(1)} fusion(f32[4,16,128,128]{3,2,1,0:T(8,128)} %fusion.7, f32[3,16,128,128]{3,2,1,0:T(8,128)} %slice.20, f32[16,128,128]{2,1,0:T(8,128)S(1)} %get-tuple-element.28, f32[4,128,16,128]{1,3,2,0:T(8,128)} %bitcast.62), kind=kOutput, calls=%fused_computation.25 | convolution fusion | flops 277872640 | bytes 14680064 | tf_op jit(solution)/shard_map/...htd,...hde->...hte/dot_general | solution.py:30
  197.6 1.4 copy.19
  198.9 0.5 copy.25
  199.5 2.2 fusion.3
  201.7 1.2 fusion.23
  202.8 1.5 collective-permute-start
  204.3 0.0 collective-permute-start.1
  204.3 0.6 collective-permute-start.2
  204.9 13.8 %collective-permute-done = bf16[128,2048]{1,0:T(8,128)(2,1)S(1)} collective-permute-done((bf16[128,2048]{1,0:T(8,128)(2,1)}, bf16[128,2048]{1,0:T(8,128)(2,1)S(1)}, u32[]{:S(2)}, u32[]{:S(2)}) %collective-permute-start) | collective-permute-done | bytes 524320 | tf_op jit(solution)/shard_map/ppermute | solution.py:82
  218.8 30.3 %collective-permute-done.1 = bf16[128,2048]{1,0:T(8,128)(2,1)S(1)} collective-permute-done((bf16[128,2048]{1,0:T(8,128)(2,1)}, bf16[128,2048]{1,0:T(8,128)(2,1)S(1)}, u32[]{:S(2)}, u32[]{:S(2)}) %collective-permute-start.1) | collective-permute-done | bytes 524320 | tf_op jit(solution)/shard_map/ppermute | solution.py:82
  249.1 0.0 copy-start.4
  249.1 0.0 collective-permute-done.2
  249.1 1.1 constant_dynamic-update-slice_fusion.3
  250.3 1.1 constant_dynamic-update-slice_fusion
  251.5 0.5 fusion
  252.0 0.0 copy-done.4
  252.0 1.9 fusion.4
  (8 shorter events, 0.3 us)
Async XLA Ops:
  10.6 53.1 %all-to-all-start.2 = ((bf16[128,4,2048]{0,2,1:T(8,128)(2,1)}), bf16[128,4,2048]{0,2,1:T(8,128)(2,1)S(1)}, u32[]{:S(2)}, u32[]{:S(2)}) async-start(bf16[128,4,2048]{0,2,1:T(8,128)(2,1)} %bitcast.55), calls=%async_computation.2 | async-start | bytes 4194304 | tf_op jit(solution)/shard_map/all_to_all | solution.py:55
  63.7 1.3 copy-start
  65.0 51.3 %all-to-all-start.1 = ((bf16[128,4,2048]{0,2,1:T(8,128)(2,1)}), bf16[128,4,2048]{0,2,1:T(8,128)(2,1)S(1)}, u32[]{:S(2)}, u32[]{:S(2)}) async-start(bf16[128,4,2048]{0,2,1:T(8,128)(2,1)} %bitcast.54), calls=%async_computation.1 | async-start | bytes 4194304 | tf_op jit(solution)/shard_map/all_to_all | solution.py:54
  68.6 119.7 %all-gather.3.cloned.1.call-start = ((), (), s32[]{:S(2)}) async-start(), calls=%async_computation.3 | async-start | bytes 5242880 | tf_op jit(solution)/shard_map/all_gather | solution.py:11
  116.3 2.4 copy-start.3
  116.5 6.5 %copy-start.1 = (f32[128,4,2048]{0,2,1:T(8,128)}, f32[128,4,2048]{0,2,1:T(8,128)S(1)}, u32[]{:S(2)}) copy-start(f32[128,4,2048]{0,2,1:T(8,128)S(1)} %convert_element_type.64) | copy-start | bytes 12582916
  118.7 4.4 %copy-start.2 = (bf16[1,128,8192]{2,1,0:T(8,128)(2,1)S(1)}, bf16[1,128,8192]{2,1,0:T(8,128)(2,1)}, u32[]{:S(2)}) copy-start(bf16[1,128,8192]{2,1,0:T(8,128)(2,1)} %param.6) | copy-start | bytes 6291460
  125.5 51.3 %all-to-all-start = ((bf16[128,4,2048]{0,2,1:T(8,128)(2,1)}), bf16[128,4,2048]{0,2,1:T(8,128)(2,1)S(1)}, u32[]{:S(2)}, u32[]{:S(2)}) async-start(bf16[128,4,2048]{0,2,1:T(8,128)(2,1)} %bitcast.52), calls=%async_computation | async-start | bytes 4194304 | tf_op jit(solution)/shard_map/all_to_all | solution.py:53
  202.8 15.9 %collective-permute-start = (bf16[128,2048]{1,0:T(8,128)(2,1)}, bf16[128,2048]{1,0:T(8,128)(2,1)S(1)}, u32[]{:S(2)}, u32[]{:S(2)}) collective-permute-start(bf16[128,2048]{1,0:T(8,128)(2,1)} %get-tuple-element.39), channel_id=1, source_target_pairs={{0,12},{4,0},{8,4},{12,8},{1,13},{5,1},{9,5},{13,9},{2,14},{6,2},{... | collective-permute-start | bytes 1572872 | tf_op jit(solution)/shard_map/ppermute | solution.py:82
  204.3 44.8 %collective-permute-start.1 = (bf16[128,2048]{1,0:T(8,128)(2,1)}, bf16[128,2048]{1,0:T(8,128)(2,1)S(1)}, u32[]{:S(2)}, u32[]{:S(2)}) collective-permute-start(bf16[128,2048]{1,0:T(8,128)(2,1)} %get-tuple-element.38), channel_id=1, source_target_pairs={{0,8},{4,12},{8,0},{12,4},{1,9},{5,13},{9,1},{13,5},{2,10},{6,14},... | collective-permute-start | bytes 1572872 | tf_op jit(solution)/shard_map/ppermute | solution.py:82
  204.3 44.8 %collective-permute-start.2 = (bf16[128,2048]{1,0:T(8,128)(2,1)}, bf16[128,2048]{1,0:T(8,128)(2,1)}, u32[]{:S(2)}, u32[]{:S(2)}) collective-permute-start(bf16[128,2048]{1,0:T(8,128)(2,1)} %get-tuple-element.37), channel_id=1, source_target_pairs={{0,4},{4,8},{8,12},{12,0},{1,5},{5,9},{9,13},{13,1},{2,6},{6,10},{... | collective-permute-start | bytes 1572872 | tf_op jit(solution)/shard_map/ppermute | solution.py:82
  249.1 2.9 %copy-start.4 = (f32[8192]{0:T(1024)S(1)}, f32[8192]{0:T(1024)}, u32[]{:S(2)}) copy-start(f32[8192]{0:T(1024)} %param.9) | copy-start | bytes 98308
Sparse Core Ops, SparseCore 0:
  123.2 32.4 all-gather.2
